TPU v7x, 32 devices: a whole 2x2x4 slice. The times are simulated.
32 devices in a mesh: tile: 16 (over z, y, x), band: 2 (over core).
Axes of the slice: x: 2, y: 2, z: 4, core: 2. Of those that a mesh axis runs over, the one named last changes fastest.
Arguments:
- voxel_feat: bfloat16 [4096, 64, 256], P(('tile', 'band')), may hold values from -6 to 6
- window_count: int32 [4096], P(('tile', 'band')), may hold values from 1 to 64
- voxel_cell: int32 [4096, 64], P(('tile', 'band')), may hold values from 0 to 2047
- w_qkv_voxel: bfloat16 [256, 768], replicated, may hold values from -1 to 1
- w_out_voxel: bfloat16 [256, 256], replicated, may hold values from -0.375 to 0.375
- w_up_voxel: bfloat16 [256, 512], replicated, may hold values from -0.375 to 0.375
- w_down_voxel: bfloat16 [512, 256], replicated, may hold values from -0.25 to 0.25
- conv_taps: float32 [9, 256], replicated, may hold values from -2 to 2
- w_qkv_bev: bfloat16 [256, 768], replicated, may hold values from -1 to 1
- w_out_bev: bfloat16 [256, 256], replicated, may hold values from -0.375 to 0.375
- w_up_bev: bfloat16 [256, 512], replicated, may hold values from -0.375 to 0.375
- w_down_bev: bfloat16 [512, 256], replicated, may hold values from -0.25 to 0.25
Outputs:
- bev_out: bfloat16 [256, 128, 256], P(('tile', 'band'))
Inputs may be any that keep to these rules, and one draw needn't show every extreme that they name: The live slots of a window are its first window_count slots. `voxel_cell`: read only for live slots.
All inputs are finite; a program needn't handle non-finite values.
Results may differ from a plain program's by a relative error of at most 0.035.
Values may be sent and summed in bfloat16 or wider, within the bound.
A program may use at most 192 MiB of HBM per device.

v0:
```python
import functools
import math

import jax
import jax.numpy as jnp
from jax import lax
from jax.experimental import pallas as pl
from jax.experimental.pallas import tpu as pltpu
from jax.sharding import PartitionSpec as P

HEADS = 8
WSIDE = 8
CB = 8
LANES = 128


def layer_norm(values, axis=-1):
    center = values - jnp.mean(values, axis=axis, keepdims=True)
    spread = jnp.mean(center * center, axis=axis, keepdims=True)
    return center * lax.rsqrt(spread + 1e-05)


def dot(a, b, contract=(1, 0)):
    return lax.dot_general(
        a, b, (((contract[0],), (contract[1],)), ((), ())), preferred_element_type=jnp.float32
    )


def attend_columns(x, counts, w_qv, w_k, w_out, w_up, w_down):
    tokens, width = x.shape
    head_dim = width // HEADS
    half_heads = LANES // head_dim
    slots = LANES // 2
    factor = head_dim ** (-0.5) * math.log2(math.e)
    turned = dot(w_qv, x, (1, 1))
    queries = turned[:width].astype(jnp.bfloat16)
    vals = turned[width:]
    keys = dot(x, w_k).astype(jnp.bfloat16)
    lane = lax.broadcasted_iota(jnp.int32, (LANES, LANES), 1)
    row = lax.broadcasted_iota(jnp.int32, (LANES, LANES), 0)
    first = lane < slots
    first_b = first.astype(jnp.bfloat16)
    second_b = 1 - first_b
    key_head = lane[:slots] // head_dim
    key_masks = [(key_head == h).astype(jnp.bfloat16) for h in range(half_heads)]
    val_masks = [(row // head_dim == h).astype(jnp.bfloat16) for h in range(half_heads)]
    mixed = []
    for pair in range(tokens // LANES):
        at = pair * LANES
        if counts is not None:
            limit = jnp.where(first[:slots], counts(2 * pair), counts(2 * pair + 1))
            bias = jnp.where(row[:slots] < limit, 0.0, -1e30)
        halves = []
        for half in range(width // LANES):
            f = half * LANES
            q = queries[f : f + LANES, at : at + LANES]
            q_blocks = jnp.concatenate([q * first_b, q * second_b], axis=0)
            k_blocks = jnp.concatenate(
                [
                    jnp.concatenate(
                        [
                            keys[at + w * slots : at + (w + 1) * slots, f : f + LANES] * m
                            for m in key_masks
                        ],
                        axis=0,
                    )
                    for w in range(2)
                ],
                axis=1,
            )
            scores = dot(k_blocks, q_blocks).reshape(half_heads, slots, LANES)
            if counts is not None:
                scores = scores + bias[None]
            top = jnp.max(scores, axis=1, keepdims=True)
            raised = jnp.exp2((scores - top) * factor)
            total = jnp.sum(raised, axis=1, keepdims=True)
            weights = raised.astype(jnp.bfloat16).reshape(half_heads * slots, LANES)
            v = vals[f : f + LANES, at : at + LANES].astype(jnp.bfloat16)
            v_blocks = jnp.concatenate([v * m for m in val_masks], axis=1)
            spread = jnp.concatenate(
                [
                    weights[h * slots : (h + 1) * slots] * m
                    for h in range(half_heads)
                    for m in (first_b[:slots], second_b[:slots])
                ],
                axis=0,
            )
            out = dot(v_blocks, spread)
            out = out.reshape(half_heads, head_dim, LANES) / total
            halves.append(out.reshape(LANES, LANES).astype(jnp.bfloat16))
        mixed.append(jnp.concatenate(halves, axis=0))
    mixed = jnp.concatenate(mixed, axis=1)
    projected = dot(w_out, mixed)
    hidden = layer_norm(x.astype(jnp.float32).T + projected, 0).astype(jnp.bfloat16)
    lifted = jax.nn.relu(dot(w_up, hidden)).astype(jnp.bfloat16)
    lowered = dot(w_down, lifted)
    return layer_norm(hidden.astype(jnp.float32) + lowered, 0)


def turn_weights(qkv_ref, out_ref, up_ref, down_ref, qv_s, out_s, up_s, down_s):
    width = out_ref.shape[0]

    def turned(values):
        return values.astype(jnp.float32).T.astype(jnp.bfloat16)

    qv_s[:width, :] = turned(qkv_ref[:, :width])
    qv_s[width:, :] = turned(qkv_ref[:, 2 * width :])
    out_s[...] = turned(out_ref[...])
    up_s[...] = turned(up_ref[...])
    down_s[...] = turned(down_ref[...])


def turned_scratch(w_qkv, w_out, w_up, w_down):
    width = w_out.shape[0]
    return [
        pltpu.VMEM((2 * width, width), jnp.bfloat16),
        pltpu.VMEM(w_out.shape[::-1], jnp.bfloat16),
        pltpu.VMEM(w_up.shape[::-1], jnp.bfloat16),
        pltpu.VMEM(w_down.shape[::-1], jnp.bfloat16),
    ]


def whole(array):
    return pl.BlockSpec(array.shape, lambda *_: (0,) * array.ndim)


def voxel_kernel(
    count_ref, x_ref, qkv_ref, out_ref, up_ref, down_ref, enc_ref, qv_s, out_s, up_s, down_s
):
    step = pl.program_id(0)
    per_step = x_ref.shape[0] * 2 // LANES
    width = x_ref.shape[1]

    @pl.when(step == 0)
    def _():
        turn_weights(qkv_ref, out_ref, up_ref, down_ref, qv_s, out_s, up_s, down_s)

    enc_ref[...] = attend_columns(
        x_ref[...],
        lambda w: count_ref[step * per_step + w],
        qv_s[...],
        qkv_ref[:, width : 2 * width],
        out_s[...],
        up_s[...],
        down_s[...],
    ).T.astype(jnp.bfloat16)


def voxel_block(feat, counts, weights):
    tokens, width = feat.shape
    size = min(512, tokens)
    steps = tokens // size
    return pl.pallas_call(
        voxel_kernel,
        grid_spec=pltpu.PrefetchScalarGridSpec(
            num_scalar_prefetch=1,
            grid=(steps,),
            in_specs=[pl.BlockSpec((size, width), lambda i, c: (i, 0))]
            + [whole(w) for w in weights],
            out_specs=pl.BlockSpec((size, width), lambda i, c: (i, 0)),
            scratch_shapes=turned_scratch(*weights),
        ),
        out_shape=jax.ShapeDtypeStruct((tokens, width), jnp.bfloat16),
        name="voxel_block",
    )(counts, feat, *weights)


def pool_kernel(
    n_tile,
    n_band,
    cell_ref,
    enc_ref,
    grid_ref,
    low_ref,
    high_ref,
    acc,
    mine,
    theirs,
    came,
    ready,
    landed,
    low,
    high,
    swap_send,
    swap_recv,
    send,
    recv,
    halo_send,
    halo_recv,
):
    tile = lax.axis_index("tile")
    band = lax.axis_index("band")
    other = 1 - band
    strip = tile * n_band + band
    chunks, _, size = cell_ref.shape
    width = enc_ref.shape[1]
    blocks = mine.shape[0]
    per = n_tile // blocks
    cells = WSIDE * CB
    block = acc.shape[0]
    mesh_id = pl.DeviceIdType.MESH

    def strip_id(s):
        return (s // n_band, s % n_band)

    barrier = pltpu.get_barrier_semaphore()

    def greet(i, carry):
        peer = lax.rem(tile + i, n_tile)
        pl.semaphore_signal(barrier, inc=1, device_id=(peer, band), device_id_type=mesh_id)
        return carry

    lax.fori_loop(1, n_tile, greet, 0)
    pl.semaphore_signal(barrier, inc=1, device_id=(tile, other), device_id_type=mesh_id)
    across_below = jnp.logical_and(band == 0, tile > 0)
    across_above = jnp.logical_and(band == n_band - 1, tile < n_tile - 1)

    @pl.when(across_below)
    def _():
        pl.semaphore_signal(barrier, inc=1, device_id=strip_id(strip - 1), device_id_type=mesh_id)

    @pl.when(across_above)
    def _():
        pl.semaphore_signal(barrier, inc=1, device_id=strip_id(strip + 1), device_id_type=mesh_id)

    across = jnp.logical_or(across_below, across_above)

    @pl.when(across)
    def _():
        pl.semaphore_wait(barrier, n_tile + 1)

    @pl.when(jnp.logical_not(across))
    def _():
        pl.semaphore_wait(barrier, n_tile)

    row = lax.broadcasted_iota(jnp.int32, (block, size), 0)

    def place(i):
        ahead = jnp.where(i < blocks - blocks // 2, blocks // 2 + i, blocks - 1 - i)
        return lax.rem(tile // per + ahead, blocks)

    def swap(j):
        return pltpu.make_async_remote_copy(
            src_ref=theirs.at[j],
            dst_ref=came.at[j],
            send_sem=swap_send.at[j],
            recv_sem=swap_recv.at[j],
            device_id=(tile, other),
            device_id_type=mesh_id,
        )

    def deliver(dest, source):
        return pltpu.make_async_remote_copy(
            src_ref=ready.at[dest],
            dst_ref=landed.at[source],
            send_sem=send.at[dest],
            recv_sem=recv.at[source],
            device_id=(dest, band),
            device_id_type=mesh_id,
        )

    def compute(i):
        j = place(i)
        acc[...] = jnp.zeros_like(acc)
        together = math.gcd(chunks, 8)

        def add(c, carry):
            term = None
            for k in range(together):
                hot = jnp.where(row == cell_ref[together * c + k] - j * block, 1.0, 0.0)
                at = pl.multiple_of((together * c + k) * size, size)
                part = dot(hot.astype(jnp.bfloat16), enc_ref[pl.ds(at, size), :])
                term = part if term is None else term + part
            acc[...] += term
            return carry

        lax.fori_loop(0, chunks // together, add, 0)
        for d in range(per):
            at = d * n_band * cells
            mine[j, d * cells : (d + 1) * cells, :] = acc[
                pl.ds(pl.multiple_of(at + band * cells, cells), cells), :
            ].astype(jnp.bfloat16)
            theirs[j, d * cells : (d + 1) * cells, :] = acc[
                pl.ds(pl.multiple_of(at + other * cells, cells), cells), :
            ].astype(jnp.bfloat16)
        swap(j).start()

    def finish(i):
        j = place(i)
        swap(j).wait_recv()
        total = mine[j].astype(jnp.float32) + came[j].astype(jnp.float32)
        normal = layer_norm(total).reshape(per, WSIDE, CB, width).astype(jnp.bfloat16)
        for d in range(per):
            dest = j * per + d

            @pl.when(dest != tile)
            def _():
                ready[dest] = normal[d]
                deliver(dest, tile).start()

            @pl.when(dest == tile)
            def _():
                landed[tile] = normal[d]

    compute(0)

    def both(i, carry):
        compute(i)
        finish(i - 1)
        return carry

    lax.fori_loop(1, blocks, both, 0)
    finish(blocks - 1)

    def arrive(i, carry):
        peer = lax.rem(tile + i, n_tile)
        deliver(peer, peer).wait_recv()
        return carry

    lax.fori_loop(1, n_tile, arrive, 0)

    def edge(side, target):
        return pltpu.make_async_remote_copy(
            src_ref=landed.at[:, 0 if side == 0 else WSIDE - 1],
            dst_ref=high if side == 0 else low,
            send_sem=halo_send.at[side],
            recv_sem=halo_recv.at[side],
            device_id=strip_id(target),
            device_id_type=mesh_id,
        )

    has_below = strip > 0
    has_above = strip < n_tile * n_band - 1

    @pl.when(has_below)
    def _():
        edge(0, strip - 1).start()

    @pl.when(has_above)
    def _():
        edge(1, strip + 1).start()

    grid_ref[...] = landed[...]

    def left(i, carry):
        peer = lax.rem(tile + i, n_tile)
        deliver(peer, peer).wait_send()
        return carry

    lax.fori_loop(1, n_tile, left, 0)

    def swapped(j, carry):
        swap(j).wait_send()
        return carry

    lax.fori_loop(0, blocks, swapped, 0)

    @pl.when(has_below)
    def _():
        edge(0, strip - 1).wait_send()
        edge(1, strip - 1).wait_recv()
        low_ref[...] = low[...]

    @pl.when(has_above)
    def _():
        edge(1, strip + 1).wait_send()
        edge(0, strip + 1).wait_recv()
        high_ref[...] = high[...]

    @pl.when(strip == 0)
    def _():
        low_ref[...] = jnp.zeros_like(low_ref)

    @pl.when(strip == n_tile * n_band - 1)
    def _():
        high_ref[...] = jnp.zeros_like(high_ref)


def pool_exchange(encoded, target, n_tile, n_band):
    tokens, width = encoded.shape
    size = min(512, tokens)
    chunks = tokens // size
    cells = WSIDE * CB
    per = math.gcd(n_tile, 4)
    blocks = n_tile // per
    half = jnp.bfloat16
    vmem = pl.BlockSpec(memory_space=pltpu.VMEM)
    return pl.pallas_call(
        functools.partial(pool_kernel, n_tile, n_band),
        in_specs=[vmem] * 2,
        out_specs=[vmem] * 3,
        out_shape=[
            jax.ShapeDtypeStruct((n_tile, WSIDE, CB, width), half),
            jax.ShapeDtypeStruct((n_tile, CB, width), half),
            jax.ShapeDtypeStruct((n_tile, CB, width), half),
        ],
        scratch_shapes=[
            pltpu.VMEM((per * n_band * cells, width), jnp.float32),
            pltpu.VMEM((blocks, per * cells, width), half),
            pltpu.VMEM((blocks, per * cells, width), half),
            pltpu.VMEM((blocks, per * cells, width), half),
            pltpu.VMEM((n_tile, WSIDE, CB, width), half),
            pltpu.VMEM((n_tile, WSIDE, CB, width), half),
            pltpu.VMEM((n_tile, CB, width), half),
            pltpu.VMEM((n_tile, CB, width), half),
            pltpu.SemaphoreType.DMA((blocks,)),
            pltpu.SemaphoreType.DMA((blocks,)),
            pltpu.SemaphoreType.DMA((n_tile,)),
            pltpu.SemaphoreType.DMA((n_tile,)),
            pltpu.SemaphoreType.DMA((2,)),
            pltpu.SemaphoreType.DMA((2,)),
        ],
        compiler_params=pltpu.CompilerParams(collective_id=0, has_side_effects=True),
        name="pool_exchange",
    )(target.reshape(chunks, 1, size), encoded)


def bev_kernel(
    grid_ref,
    low_ref,
    high_ref,
    tap_ref,
    qkv_ref,
    out_ref,
    up_ref,
    down_ref,
    result_ref,
    wide,
    qv_s,
    out_s,
    up_s,
    down_s,
):
    step = pl.program_id(0)
    n_tile, _, _, width = grid_ref.shape
    span = result_ref.shape[1]

    @pl.when(step == 0)
    def _():
        turn_weights(qkv_ref, out_ref, up_ref, down_ref, qv_s, out_s, up_s, down_s)
        edge = jnp.zeros((WSIDE + 2, CB, width), jnp.float32)
        wide[:, :CB, :] = edge
        wide[:, (n_tile + 1) * CB :, :] = edge

        def fill(t, carry):
            to = pl.ds(pl.multiple_of((t + 1) * CB, CB), CB)
            wide[0, to, :] = low_ref[t].astype(jnp.float32)
            wide[WSIDE + 1, to, :] = high_ref[t].astype(jnp.float32)
            wide[1 : WSIDE + 1, to, :] = grid_ref[t].astype(jnp.float32)
            return carry

        lax.fori_loop(0, n_tile, fill, 0)

    at = pl.multiple_of(step * span, span)
    sums = [jnp.zeros((span, width), jnp.float32) for _ in range(WSIDE)]
    centers = []
    for r in range(WSIDE + 2):
        slab = wide[r, pl.ds(at, span + 2 * CB), :]
        for c in range(3):
            moved = slab[CB + c - 1 : CB + c - 1 + span]
            if c == 1:
                centers.append(moved)
            for row_tap in range(3):
                to = r - row_tap
                if 0 <= to < WSIDE:
                    tap = tap_ref[3 * row_tap + c : 3 * row_tap + c + 1, :]
                    sums[to] = sums[to] + moved * tap
    shaped = [centers[r + 1] + sums[r] for r in range(WSIDE)]
    count = span // CB
    x = jnp.concatenate(
        [shaped[r][w * CB : (w + 1) * CB] for w in range(count) for r in range(WSIDE)], axis=0
    ).astype(jnp.bfloat16)
    result = attend_columns(
        x, None, qv_s[...], qkv_ref[:, width : 2 * width], out_s[...], up_s[...], down_s[...]
    ).T
    for r in range(WSIDE):
        result_ref[r] = jnp.concatenate(
            [result[(w * WSIDE + r) * CB : (w * WSIDE + r + 1) * CB] for w in range(count)], axis=0
        ).astype(jnp.bfloat16)


def bev_block(grid, low, high, taps, weights):
    n_tile, _, _, width = grid.shape
    cols = n_tile * CB
    span = min(64, cols)
    inputs = (grid, low, high, taps, *weights)
    return pl.pallas_call(
        bev_kernel,
        grid=(cols // span,),
        in_specs=[whole(a) for a in inputs],
        out_specs=pl.BlockSpec((WSIDE, span, width), lambda i: (0, i, 0)),
        out_shape=jax.ShapeDtypeStruct((WSIDE, cols, width), jnp.bfloat16),
        scratch_shapes=[pltpu.VMEM((WSIDE + 2, cols + 2 * CB, width), jnp.float32)]
        + turned_scratch(*weights),
        name="bev_block",
    )(*inputs)


def shards(
    voxel_feat,
    window_count,
    voxel_cell,
    w_qkv_voxel,
    w_out_voxel,
    w_up_voxel,
    w_down_voxel,
    conv_taps,
    w_qkv_bev,
    w_out_bev,
    w_up_bev,
    w_down_bev,
):
    n_tile = lax.axis_size("tile")
    n_band = lax.axis_size("band")
    width = voxel_feat.shape[2]
    slot_ids = jnp.arange(voxel_feat.shape[1], dtype=jnp.int32)
    keep = slot_ids[None, :] < window_count[:, None]
    target = jnp.where(keep, voxel_cell, -1)
    encoded = voxel_block(
        voxel_feat.reshape(-1, width),
        window_count,
        (w_qkv_voxel, w_out_voxel, w_up_voxel, w_down_voxel),
    )
    grid, low, high = pool_exchange(encoded, target, n_tile, n_band)
    return bev_block(
        grid, low, high, conv_taps, (w_qkv_bev, w_out_bev, w_up_bev, w_down_bev)
    )


def solution(mesh):
    placed = (
        P(("tile", "band"), None, None),
        P(("tile", "band")),
        P(("tile", "band"), None),
        P(),
        P(),
        P(),
        P(),
        P(),
        P(),
        P(),
        P(),
        P(),
    )
    return jax.shard_map(
        shards,
        mesh=mesh,
        in_specs=placed,
        out_specs=P(("tile", "band"), None, None),
        check_vma=False,
    )
```

profile of v0, /device:TPU:11, one launch (start us, length us, event | category | flops | bytes accessed | tf_op | source)
XLA Modules:
  0.0 77.2 jit_solution(12502084813596541040)
XLA Ops:
  0.0 0.8 fusion
  0.8 0.1 copy.14
  0.9 0.7 reshape.9.cell_ref
  1.6 38.3 %voxel_block.1.enc_ref = bf16[8192,256]{1,0:T(8,128)(2,1)} custom-call(s32[128]{0:T(128)} %count_ref.1, bf16[8192,256]{1,0:T(8,128)(2,1)} %bitcast.1, bf16[256,768]{1,0:T(8,128)(2,1)} %qkv_ref.2, bf16[256,256]{1,0:T(8,128)(2,1)} %out_ref.2, bf16[256,512]{1,0:T(8,128)(2,1)} %up_ref.2, bf16[512,256]{1,0:T(8,128)(2,1)} %down_ref.2), custom_call_target="tpu_custom_call" | custom-call | tf_op jit(solution)/shard_map/voxel_block/pallas_call | solution.py:153
  39.8 29.3 %pool_exchange.1 = (bf16[16,8,8,256]{3,2,1,0:T(8,128)(2,1)}, bf16[16,8,256]{2,1,0:T(8,128)(2,1)}, bf16[16,8,256]{2,1,0:T(8,128)(2,1)}) custom-call(s32[16,1,512]{2,1,0:T(1,128)} %reshape.9.cell_ref, bf16[8192,256]{1,0:T(8,128)(2,1)} %voxel_block.1.enc_ref), custom_call_target="tpu_custom_call" | custom-call | tf_op jit(solution)/shard_map/pool_exchange/pallas_call | solution.py:388
  69.2 8.1 %bev_block.1 = bf16[8,128,256]{2,1,0:T(8,128)(2,1)} custom-call(bf16[16,8,8,256]{3,2,1,0:T(8,128)(2,1)} %get-tuple-element.8.grid_ref, bf16[16,8,256]{2,1,0:T(8,128)(2,1)} %get-tuple-element.9.low_ref, bf16[16,8,256]{2,1,0:T(8,128)(2,1)} %get-tuple-element.10.high_ref, f32[9,256]{1,0:T(8,128)} %tap_ref.1, bf16[256,768]{1,0:T(8,128)(2,1)} %qkv_ref.3, ...), custom_call_target="tpu_custom_call" | custom-call | tf_op jit(solution)/shard_map/bev_block/pallas_call | solution.py:487
where the time goes:
time: 78.5 us; the launch traced here: 77.2 us
  Pallas kernels  75.6 us (96%)
  local copies, waits for them, and re-layouts  0.81 us (1%)
    pallas_call x1, Pallas kernels, voxel_block(): pl.pallas_call(voxel_kernel, grid_spec=pltpu.PrefetchScalarGridSpec(num_s...  38.3 us
    pallas_call x1, Pallas kernels, pool_exchange(): pl.pallas_call(functools.partial(pool_kernel, n_tile, n_band), in_specs=[...  29.3 us
    pallas_call x1, Pallas kernels, bev_block(): pl.pallas_call(bev_kernel, grid=(cols // span,), in_specs=[whole(a) for a...  8.06 us

commit v1 on v0

--- a/solution.py
+++ b/solution.py
@@ -12,6 +12,8 @@
 WSIDE = 8
 CB = 8
 LANES = 128
+CHUNK = 8
+GROUP = 4
 
 
 def layer_norm(values, axis=-1):
@@ -26,71 +28,95 @@
     )
 
 
-def attend_columns(x, counts, w_qv, w_k, w_out, w_up, w_down):
-    tokens, width = x.shape
-    head_dim = width // HEADS
-    half_heads = LANES // head_dim
-    slots = LANES // 2
-    factor = head_dim ** (-0.5) * math.log2(math.e)
-    turned = dot(w_qv, x, (1, 1))
-    queries = turned[:width].astype(jnp.bfloat16)
-    vals = turned[width:]
-    keys = dot(x, w_k).astype(jnp.bfloat16)
-    lane = lax.broadcasted_iota(jnp.int32, (LANES, LANES), 1)
-    row = lax.broadcasted_iota(jnp.int32, (LANES, LANES), 0)
-    first = lane < slots
-    first_b = first.astype(jnp.bfloat16)
-    second_b = 1 - first_b
-    key_head = lane[:slots] // head_dim
-    key_masks = [(key_head == h).astype(jnp.bfloat16) for h in range(half_heads)]
-    val_masks = [(row // head_dim == h).astype(jnp.bfloat16) for h in range(half_heads)]
-    mixed = []
-    for pair in range(tokens // LANES):
-        at = pair * LANES
-        if counts is not None:
-            limit = jnp.where(first[:slots], counts(2 * pair), counts(2 * pair + 1))
-            bias = jnp.where(row[:slots] < limit, 0.0, -1e30)
-        halves = []
-        for half in range(width // LANES):
-            f = half * LANES
-            q = queries[f : f + LANES, at : at + LANES]
-            q_blocks = jnp.concatenate([q * first_b, q * second_b], axis=0)
-            k_blocks = jnp.concatenate(
-                [
-                    jnp.concatenate(
-                        [
-                            keys[at + w * slots : at + (w + 1) * slots, f : f + LANES] * m
-                            for m in key_masks
-                        ],
-                        axis=0,
-                    )
-                    for w in range(2)
-                ],
-                axis=1,
-            )
-            scores = dot(k_blocks, q_blocks).reshape(half_heads, slots, LANES)
-            if counts is not None:
-                scores = scores + bias[None]
-            top = jnp.max(scores, axis=1, keepdims=True)
-            raised = jnp.exp2((scores - top) * factor)
-            total = jnp.sum(raised, axis=1, keepdims=True)
-            weights = raised.astype(jnp.bfloat16).reshape(half_heads * slots, LANES)
-            v = vals[f : f + LANES, at : at + LANES].astype(jnp.bfloat16)
-            v_blocks = jnp.concatenate([v * m for m in val_masks], axis=1)
-            spread = jnp.concatenate(
-                [
-                    weights[h * slots : (h + 1) * slots] * m
-                    for h in range(half_heads)
-                    for m in (first_b[:slots], second_b[:slots])
-                ],
-                axis=0,
-            )
-            out = dot(v_blocks, spread)
-            out = out.reshape(half_heads, head_dim, LANES) / total
-            halves.append(out.reshape(LANES, LANES).astype(jnp.bfloat16))
-        mixed.append(jnp.concatenate(halves, axis=0))
-    mixed = jnp.concatenate(mixed, axis=1)
-    projected = dot(w_out, mixed)
+class Mixer:
+    def __init__(self, tokens, width, bias_of=None):
+        self.tokens, self.width, self.bias_of = tokens, width, bias_of
+        self.head_dim = width // HEADS
+        self.heads = LANES // self.head_dim
+        self.slots = LANES // 2
+        lane = lax.broadcasted_iota(jnp.int32, (LANES, LANES), 1)
+        row = lax.broadcasted_iota(jnp.int32, (LANES, LANES), 0)
+        self.first = (lane < self.slots).astype(jnp.bfloat16)
+        self.second = 1 - self.first
+        key_head = lane[: self.slots] // self.head_dim
+        self.key_masks = [(key_head == h).astype(jnp.bfloat16) for h in range(self.heads)]
+        self.val_masks = [
+            (row // self.head_dim == h).astype(jnp.bfloat16) for h in range(self.heads)
+        ]
+        self.units = [
+            (pair, half) for pair in range(tokens // LANES) for half in range(width // LANES)
+        ]
+        self.scored = {}
+        self.parts = {}
+        self.biases = {}
+
+    def turn(self, x, w_qv):
+        turned = dot(w_qv, x, (1, 1))
+        self.queries = turned[: self.width].astype(jnp.bfloat16)
+        self.vals = turned[self.width :].astype(jnp.bfloat16)
+
+    def key(self, x, w_k):
+        self.keys = dot(x, w_k).astype(jnp.bfloat16)
+
+    def score(self, unit):
+        pair, half = unit
+        at, f, slots = pair * LANES, half * LANES, self.slots
+        q = self.queries[f : f + LANES, at : at + LANES]
+        q_blocks = jnp.concatenate([q * self.first, q * self.second], axis=0)
+        sides = []
+        for w in range(2):
+            k = self.keys[at + w * slots : at + (w + 1) * slots, f : f + LANES]
+            sides.append(jnp.concatenate([k * m for m in self.key_masks], axis=0))
+        k_blocks = jnp.concatenate(sides, axis=1)
+        scores = dot(k_blocks, q_blocks).reshape(self.heads, slots, LANES)
+        if self.bias_of is not None:
+            if pair not in self.biases:
+                self.biases[pair] = self.bias_of(pair)
+            scores = scores + self.biases[pair][None]
+        self.scored[unit] = scores
+
+    def mix(self, unit):
+        pair, half = unit
+        at, f, slots = pair * LANES, half * LANES, self.slots
+        factor = self.head_dim ** (-0.5) * math.log2(math.e)
+        scores = self.scored.pop(unit)
+        top = jnp.max(scores, axis=1, keepdims=True)
+        raised = jnp.exp2((scores - top) * factor)
+        total = jnp.sum(raised, axis=1, keepdims=True)
+        weights = raised.astype(jnp.bfloat16)
+        v = self.vals[f : f + LANES, at : at + LANES]
+        v_blocks = jnp.concatenate([v * m for m in self.val_masks], axis=1)
+        spread = jnp.concatenate(
+            [
+                weights[h] * m
+                for h in range(self.heads)
+                for m in (self.first[:slots], self.second[:slots])
+            ],
+            axis=0,
+        )
+        out = dot(v_blocks, spread)
+        out = out.reshape(self.heads, self.head_dim, LANES) / total
+        self.parts[unit] = out.reshape(LANES, LANES).astype(jnp.bfloat16)
+
+    def mixed(self):
+        pairs, halves = self.tokens // LANES, self.width // LANES
+        return jnp.concatenate(
+            [
+                jnp.concatenate([self.parts[p, h] for h in range(halves)], axis=0)
+                for p in range(pairs)
+            ],
+            axis=1,
+        )
+
+
+def attend_columns(x, w_qv, w_k, w_out, w_up, w_down):
+    mixer = Mixer(x.shape[0], x.shape[1])
+    mixer.turn(x, w_qv)
+    mixer.key(x, w_k)
+    for unit in mixer.units:
+        mixer.score(unit)
+        mixer.mix(unit)
+    projected = dot(w_out, mixer.mixed())
     hidden = layer_norm(x.astype(jnp.float32).T + projected, 0).astype(jnp.bfloat16)
     lifted = jax.nn.relu(dot(w_up, hidden)).astype(jnp.bfloat16)
     lowered = dot(w_down, lifted)
@@ -124,58 +150,233 @@
     return pl.BlockSpec(array.shape, lambda *_: (0,) * array.ndim)
 
 
+def bin_table(counts, slots):
+    windows = counts.shape[1]
+    chunks = slots // CHUNK
+    lanes = 2 * windows
+    units = (counts + (CHUNK - 1)) // CHUNK
+    wide = lax.broadcasted_iota(jnp.int32, (windows, windows), 1)
+    key = jnp.broadcast_to(units * windows, (windows, windows)) + wide
+    key = key.astype(jnp.float32)
+    key_t = key.T
+    rank = jnp.sum(jnp.where(key < key_t, 1.0, 0.0), axis=1, keepdims=True).astype(jnp.int32)
+    count_t = jnp.broadcast_to(counts, (windows, windows)).astype(jnp.float32).T[:, :1]
+    alone = jnp.zeros((1, 1), jnp.int32)
+    for large in range(chunks // 2 + 1, chunks + 1):
+        many = jnp.sum(jnp.where(units >= large, 1, 0), axis=1, keepdims=True)
+        few = jnp.sum(jnp.where(units <= chunks - large, 1, 0), axis=1, keepdims=True)
+        alone = jnp.maximum(alone, many - few)
+    rest = windows - alone
+    pairs = (rest + 1) // 2
+    lane = lax.broadcasted_iota(jnp.int32, (1, lanes), 1)
+    paired = lane < pairs
+    rank_a = jnp.where(paired, lane, rest + lane - pairs)
+    rank_b = jnp.where(paired, rest - 1 - lane, rank_a)
+    index = lax.broadcasted_iota(jnp.int32, (windows, 1), 0).astype(jnp.float32)
+
+    def pick(ranks, values):
+        return jnp.sum(jnp.where(rank == ranks, values, 0.0), axis=0, keepdims=True).astype(jnp.int32)
+
+    win_a, win_b = pick(rank_a, index), pick(rank_b, index)
+    count_a, count_b = pick(rank_a, count_t), pick(rank_b, count_t)
+    single = rank_a == rank_b
+    size_a = jnp.where(single, chunks // 2, (count_a + (CHUNK - 1)) // CHUNK)
+    source_b = jnp.where(single, win_a * chunks + chunks // 2, win_b * chunks)
+    split = jnp.where(single, slots, size_a * CHUNK)
+    end_b = jnp.where(single, 0, split + count_b)
+    bins = jnp.broadcast_to(pairs + alone, (1, lanes))
+    return jnp.concatenate([win_a, size_a, source_b, win_b, split, count_a, end_b, bins], axis=0)
+
+
 def voxel_kernel(
-    count_ref, x_ref, qkv_ref, out_ref, up_ref, down_ref, enc_ref, qv_s, out_s, up_s, down_s
+    count_ref,
+    x_hbm,
+    cell_ref,
+    qkv_ref,
+    out_ref,
+    up_ref,
+    down_ref,
+    pooled_ref,
+    acc,
+    xbuf,
+    table_v,
+    table,
+    twice,
+    mixed_s,
+    turned_s,
+    target_s,
+    rows_s,
+    qv_s,
+    out_s,
+    up_s,
+    down_s,
+    x_sem,
+    table_sem,
 ):
-    step = pl.program_id(0)
-    per_step = x_ref.shape[0] * 2 // LANES
-    width = x_ref.shape[1]
-
-    @pl.when(step == 0)
-    def _():
-        turn_weights(qkv_ref, out_ref, up_ref, down_ref, qv_s, out_s, up_s, down_s)
-
-    enc_ref[...] = attend_columns(
-        x_ref[...],
-        lambda w: count_ref[step * per_step + w],
-        qv_s[...],
-        qkv_ref[:, width : 2 * width],
-        out_s[...],
-        up_s[...],
-        down_s[...],
-    ).T.astype(jnp.bfloat16)
-
-
-def voxel_block(feat, counts, weights):
-    tokens, width = feat.shape
-    size = min(512, tokens)
-    steps = tokens // size
+    width = out_ref.shape[0]
+    slots = cell_ref.shape[1]
+    chunks = slots // CHUNK
+    span = GROUP * slots
+    cells = acc.shape[0]
+    block = rows_s.shape[0]
+
+    table_v[...] = bin_table(count_ref[...], slots)
+    to_table = pltpu.make_async_copy(table_v, table, table_sem)
+    to_table.start()
+    turn_weights(qkv_ref, out_ref, up_ref, down_ref, qv_s, out_s, up_s, down_s)
+    twice[...] = jnp.concatenate([cell_ref[...], cell_ref[...]], axis=1)
+    to_table.wait()
+    groups = (table[7, 0] + (GROUP - 1)) // GROUP
+
+    def fetch(g, slot):
+        for k in range(GROUP):
+            b = g * GROUP + k
+            size = table[1, b]
+            at = k * chunks
+            pltpu.make_async_copy(
+                x_hbm.at[pl.ds(table[0, b] * chunks, size)],
+                xbuf.at[slot, pl.ds(at, size)],
+                x_sem.at[slot],
+            ).start()
+            pltpu.make_async_copy(
+                x_hbm.at[pl.ds(table[2, b], chunks - size)],
+                xbuf.at[slot, pl.ds(at + size, chunks - size)],
+                x_sem.at[slot],
+            ).start()
+
+    def fetched(slot):
+        pltpu.make_async_copy(
+            x_hbm.at[pl.ds(0, GROUP * chunks)], xbuf.at[slot], x_sem.at[slot]
+        ).wait()
+
+    fetch(0, 0)
+    acc[...] = jnp.zeros_like(acc)
+    mixed_s[...] = jnp.zeros_like(mixed_s)
+    turned_s[...] = jnp.zeros_like(turned_s)
+    target_s[...] = jnp.full_like(target_s, -1.0)
+    rows_s[...] = lax.broadcasted_iota(jnp.int32, rows_s.shape, 0).astype(jnp.float32).astype(jnp.bfloat16)
+
+    lane = lax.broadcasted_iota(jnp.int32, (1, LANES), 1)
+    first = lane < slots
+    place = lane % slots
+    key_row = lax.broadcasted_iota(jnp.int32, (slots, LANES), 0)
+
+    def limits_of(g):
+        limits = []
+        targets = []
+        for pair in range(span // LANES):
+            pick = []
+            for half in range(2):
+                b = g * GROUP + 2 * pair + half
+                split = table[4, b]
+                own = twice[pl.ds(table[0, b], 1), :]
+                other = twice[pl.ds(table[3, b], 1), :]
+                other = pltpu.roll(other, lax.rem(split, slots), 1)
+                pick.append(
+                    (split, table[5, b], table[6, b], jnp.where(place < split, own, other))
+                )
+            split, count, end, cell = [jnp.where(first, u, v) for u, v in zip(*pick)]
+            late = place >= split
+            low = jnp.where(late, split, 0)
+            high = jnp.where(late, end, count)
+            limits.append((low, high))
+            live = jnp.logical_and(place >= low, place < high)
+            targets.append(jnp.where(live, cell, -1).astype(jnp.float32))
+        return limits, jnp.concatenate(targets, axis=1)
+
+    def step(g, carry):
+        slot = lax.rem(g, 2)
+        fetch(g + 1, 1 - slot)
+        fetched(slot)
+        limits, next_target = limits_of(g)
+
+        def bias_of(pair):
+            low, high = limits[pair]
+            return jnp.where(jnp.logical_and(key_row >= low, key_row < high), 0.0, -1e30)
+
+        mixer = Mixer(span, width, bias_of)
+        target = target_s[...]
+        one, none = jnp.bfloat16(1), jnp.bfloat16(0)
+
+        def pool(c):
+            near = (target - float(c * block)).astype(jnp.bfloat16)
+            hot = jnp.where(rows_s[...] == near, one, none)
+            at = slice(c * block, (c + 1) * block)
+            acc[at, :] += dot(hot, encoded)
+
+        x = xbuf[slot].astype(jnp.float32).reshape(span, width)
+        x_b = x.astype(jnp.bfloat16)
+        units = mixer.units
+        mixer.turn(x_b, qv_s[...])
+        projected = dot(out_s[...], mixed_s[...])
+        mixer.key(x_b, qkv_ref[:, width : 2 * width])
+        mixer.score(units[0])
+        hidden = layer_norm(turned_s[...].astype(jnp.float32) + projected, 0).astype(jnp.bfloat16)
+        turned_s[...] = x.T.astype(jnp.bfloat16)
+        lifted = jax.nn.relu(dot(up_s[...], hidden)).astype(jnp.bfloat16)
+        mixer.score(units[1])
+        mixer.mix(units[0])
+        lowered = dot(down_s[...], lifted)
+        mixer.score(units[2])
+        mixer.mix(units[1])
+        encoded = layer_norm(hidden.astype(jnp.float32) + lowered, 0).T.astype(jnp.bfloat16)
+        mixer.score(units[3])
+        mixer.mix(units[2])
+        blocks = cells // block
+        for c in range(blocks // 2):
+            pool(c)
+        mixer.mix(units[3])
+        for c in range(blocks // 2, blocks):
+            pool(c)
+        target_s[...] = next_target
+        mixed_s[...] = mixer.mixed()
+        return carry
+
+    lax.fori_loop(0, groups + 1, step, 0)
+    fetched(lax.rem(groups + 1, 2))
+    pooled_ref[...] = acc[...].astype(jnp.bfloat16)
+
+
+def voxel_pool(feat, counts, cell, weights, cells):
+    windows, slots, width = feat.shape
+    vmem = pl.BlockSpec(memory_space=pltpu.VMEM)
+    span = GROUP * slots
+    chunks = slots // CHUNK
+    block = math.gcd(cells, 256)
     return pl.pallas_call(
         voxel_kernel,
-        grid_spec=pltpu.PrefetchScalarGridSpec(
-            num_scalar_prefetch=1,
-            grid=(steps,),
-            in_specs=[pl.BlockSpec((size, width), lambda i, c: (i, 0))]
-            + [whole(w) for w in weights],
-            out_specs=pl.BlockSpec((size, width), lambda i, c: (i, 0)),
-            scratch_shapes=turned_scratch(*weights),
-        ),
-        out_shape=jax.ShapeDtypeStruct((tokens, width), jnp.bfloat16),
-        name="voxel_block",
-    )(counts, feat, *weights)
+        in_specs=[vmem, pl.BlockSpec(memory_space=pl.ANY)] + [vmem] * 5,
+        out_specs=vmem,
+        out_shape=jax.ShapeDtypeStruct((cells, width), jnp.bfloat16),
+        scratch_shapes=[
+            pltpu.VMEM((cells, width), jnp.float32),
+            pltpu.VMEM((2, GROUP * chunks, CHUNK, width), jnp.bfloat16),
+            pltpu.VMEM((8, 2 * windows), jnp.int32),
+            pltpu.SMEM((8, 2 * windows), jnp.int32),
+            pltpu.VMEM((windows, 2 * slots), jnp.int32),
+            pltpu.VMEM((width, span), jnp.bfloat16),
+            pltpu.VMEM((width, span), jnp.bfloat16),
+            pltpu.VMEM((1, span), jnp.float32),
+            pltpu.VMEM((block, span), jnp.bfloat16),
+        ]
+        + turned_scratch(*weights)
+        + [pltpu.SemaphoreType.DMA((2,)), pltpu.SemaphoreType.DMA],
+        name="voxel_pool",
+    )(
+        counts.reshape(1, windows),
+        feat.reshape(windows * chunks, CHUNK, width),
+        cell,
+        *weights,
+    )
 
 
 def pool_kernel(
     n_tile,
     n_band,
-    cell_ref,
-    enc_ref,
+    pooled_ref,
     grid_ref,
     low_ref,
     high_ref,
-    acc,
-    mine,
-    theirs,
     came,
     ready,
     landed,
@@ -192,12 +393,10 @@
     band = lax.axis_index("band")
     other = 1 - band
     strip = tile * n_band + band
-    chunks, _, size = cell_ref.shape
-    width = enc_ref.shape[1]
-    blocks = mine.shape[0]
+    width = pooled_ref.shape[3]
+    blocks = came.shape[0]
     per = n_tile // blocks
     cells = WSIDE * CB
-    block = acc.shape[0]
     mesh_id = pl.DeviceIdType.MESH
 
     def strip_id(s):
@@ -233,15 +432,13 @@
     def _():
         pl.semaphore_wait(barrier, n_tile)
 
-    row = lax.broadcasted_iota(jnp.int32, (block, size), 0)
-
     def place(i):
         ahead = jnp.where(i < blocks - blocks // 2, blocks // 2 + i, blocks - 1 - i)
         return lax.rem(tile // per + ahead, blocks)
 
     def swap(j):
         return pltpu.make_async_remote_copy(
-            src_ref=theirs.at[j],
+            src_ref=pooled_ref.at[pl.ds(j * per, per), other],
             dst_ref=came.at[j],
             send_sem=swap_send.at[j],
             recv_sem=swap_recv.at[j],
@@ -259,36 +456,11 @@
             device_id_type=mesh_id,
         )
 
-    def compute(i):
-        j = place(i)
-        acc[...] = jnp.zeros_like(acc)
-        together = math.gcd(chunks, 8)
-
-        def add(c, carry):
-            term = None
-            for k in range(together):
-                hot = jnp.where(row == cell_ref[together * c + k] - j * block, 1.0, 0.0)
-                at = pl.multiple_of((together * c + k) * size, size)
-                part = dot(hot.astype(jnp.bfloat16), enc_ref[pl.ds(at, size), :])
-                term = part if term is None else term + part
-            acc[...] += term
-            return carry
-
-        lax.fori_loop(0, chunks // together, add, 0)
-        for d in range(per):
-            at = d * n_band * cells
-            mine[j, d * cells : (d + 1) * cells, :] = acc[
-                pl.ds(pl.multiple_of(at + band * cells, cells), cells), :
-            ].astype(jnp.bfloat16)
-            theirs[j, d * cells : (d + 1) * cells, :] = acc[
-                pl.ds(pl.multiple_of(at + other * cells, cells), cells), :
-            ].astype(jnp.bfloat16)
-        swap(j).start()
-
     def finish(i):
         j = place(i)
         swap(j).wait_recv()
-        total = mine[j].astype(jnp.float32) + came[j].astype(jnp.float32)
+        mine = pooled_ref[pl.ds(j * per, per), band].astype(jnp.float32)
+        total = mine + came[j].astype(jnp.float32)
         normal = layer_norm(total).reshape(per, WSIDE, CB, width).astype(jnp.bfloat16)
         for d in range(per):
             dest = j * per + d
@@ -302,15 +474,17 @@
             def _():
                 landed[tile] = normal[d]
 
-    compute(0)
-
-    def both(i, carry):
-        compute(i)
-        finish(i - 1)
+    def swap_start(i, carry):
+        swap(place(i)).start()
         return carry
 
-    lax.fori_loop(1, blocks, both, 0)
-    finish(blocks - 1)
+    lax.fori_loop(0, blocks, swap_start, 0)
+
+    def swap_finish(i, carry):
+        finish(i)
+        return carry
+
+    lax.fori_loop(0, blocks, swap_finish, 0)
 
     def arrive(i, carry):
         peer = lax.rem(tile + i, n_tile)
@@ -376,10 +550,8 @@
         high_ref[...] = jnp.zeros_like(high_ref)
 
 
-def pool_exchange(encoded, target, n_tile, n_band):
-    tokens, width = encoded.shape
-    size = min(512, tokens)
-    chunks = tokens // size
+def pool_exchange(pooled, n_tile, n_band):
+    cells, width = pooled.shape
     cells = WSIDE * CB
     per = math.gcd(n_tile, 4)
     blocks = n_tile // per
@@ -387,7 +559,7 @@
     vmem = pl.BlockSpec(memory_space=pltpu.VMEM)
     return pl.pallas_call(
         functools.partial(pool_kernel, n_tile, n_band),
-        in_specs=[vmem] * 2,
+        in_specs=[vmem],
         out_specs=[vmem] * 3,
         out_shape=[
             jax.ShapeDtypeStruct((n_tile, WSIDE, CB, width), half),
@@ -395,10 +567,7 @@
             jax.ShapeDtypeStruct((n_tile, CB, width), half),
         ],
         scratch_shapes=[
-            pltpu.VMEM((per * n_band * cells, width), jnp.float32),
-            pltpu.VMEM((blocks, per * cells, width), half),
-            pltpu.VMEM((blocks, per * cells, width), half),
-            pltpu.VMEM((blocks, per * cells, width), half),
+            pltpu.VMEM((blocks, per, cells, width), half),
             pltpu.VMEM((n_tile, WSIDE, CB, width), half),
             pltpu.VMEM((n_tile, WSIDE, CB, width), half),
             pltpu.VMEM((n_tile, CB, width), half),
@@ -412,7 +581,7 @@
         ],
         compiler_params=pltpu.CompilerParams(collective_id=0, has_side_effects=True),
         name="pool_exchange",
-    )(target.reshape(chunks, 1, size), encoded)
+    )(pooled.reshape(n_tile, n_band, cells, width))
 
 
 def bev_kernel(
@@ -471,7 +640,7 @@
         [shaped[r][w * CB : (w + 1) * CB] for w in range(count) for r in range(WSIDE)], axis=0
     ).astype(jnp.bfloat16)
     result = attend_columns(
-        x, None, qv_s[...], qkv_ref[:, width : 2 * width], out_s[...], up_s[...], down_s[...]
+        x, qv_s[...], qkv_ref[:, width : 2 * width], out_s[...], up_s[...], down_s[...]
     ).T
     for r in range(WSIDE):
         result_ref[r] = jnp.concatenate(
@@ -512,16 +681,14 @@
 ):
     n_tile = lax.axis_size("tile")
     n_band = lax.axis_size("band")
-    width = voxel_feat.shape[2]
-    slot_ids = jnp.arange(voxel_feat.shape[1], dtype=jnp.int32)
-    keep = slot_ids[None, :] < window_count[:, None]
-    target = jnp.where(keep, voxel_cell, -1)
-    encoded = voxel_block(
-        voxel_feat.reshape(-1, width),
+    pooled = voxel_pool(
+        voxel_feat,
         window_count,
+        voxel_cell,
         (w_qkv_voxel, w_out_voxel, w_up_voxel, w_down_voxel),
+        WSIDE * CB * n_tile * n_band,
     )
-    grid, low, high = pool_exchange(encoded, target, n_tile, n_band)
+    grid, low, high = pool_exchange(pooled, n_tile, n_band)
     return bev_block(
         grid, low, high, conv_taps, (w_qkv_bev, w_out_bev, w_up_bev, w_down_bev)
     )

time: 78.5 us -> 71.4 us (0.910)
  Pallas kernels: 75.6 us -> 69.1 us
    pallas_call x1, Pallas kernels: 29.3 us -> 25.2 us  [pool_exchange(): pl.pallas_call(functools.partial(pool_kernel, n_tile, n_band), in_specs=[...]
    pallas_call x1, Pallas kernels: 38.3 us -> 35.9 us  [voxel_pool(): pl.pallas_call(voxel_kernel, in_specs=[vmem, pl.BlockSpec(memory_space=pl...]
    unnamed x0 -> x1, local copies, waits for them, and re-layouts: none -> 1.49 us
where the time goes in v1:
time: 71.4 us; the launch traced here: 70.6 us
  Pallas kernels  69.1 us (97%)
  local copies, waits for them, and re-layouts  1.49 us (2%)
    pallas_call x1, Pallas kernels, voxel_pool(): pl.pallas_call(voxel_kernel, in_specs=[vmem, pl.BlockSpec(memory_space=pl...  35.9 us
    pallas_call x1, Pallas kernels, pool_exchange(): pl.pallas_call(functools.partial(pool_kernel, n_tile, n_band), in_specs=[...  25.2 us
    pallas_call x1, Pallas kernels, bev_block(): pl.pallas_call(bev_kernel, grid=(cols // span,), in_specs=[whole(a) for a...  8.06 us
    unnamed x1, local copies, waits for them, and re-layouts  1.49 us

profile of v1, /device:TPU:11, one launch (start us, length us, event | category | flops | bytes accessed | tf_op | source)
XLA Modules:
  0.0 70.6 jit_solution(10182776539048643908)
XLA Ops:
  0.0 1.5 %copy.13.cell_ref = s32[128,64]{1,0:T(8,128)} copy(s32[128,64]{0,1:T(8,128)} %param.14) | data formatting | bytes 65536 | tf_op args[2]
  1.5 35.9 %voxel_pool.1 = bf16[2048,256]{1,0:T(8,128)(2,1)} custom-call(s32[1,128]{1,0:T(1,128)} %bitcast.5, bf16[1024,8,256]{2,1,0:T(8,128)(2,1)} %bitcast.4, s32[128,64]{1,0:T(8,128)} %copy.13.cell_ref, bf16[256,768]{1,0:T(8,128)(2,1)} %qkv_ref.2, bf16[256,256]{1,0:T(8,128)(2,1)} %out_ref.2, bf16[256,512]{1,0:T(8,128)(2,1)} %up_ref.2, bf16[512,256]{1,0:T(8,128)(2,1)} %down_ref.2), custom_call_target="tpu_custom_call" | custom-call | tf_op jit(solution)/shard_map/voxel_pool/pallas_call | solution.py:346
  37.4 25.2 %pool_exchange.1 = (bf16[16,8,8,256]{3,2,1,0:T(8,128)(2,1)}, bf16[16,8,256]{2,1,0:T(8,128)(2,1)}, bf16[16,8,256]{2,1,0:T(8,128)(2,1)}) custom-call(bf16[16,2,64,256]{3,2,1,0:T(8,128)(2,1)} %bitcast.3), custom_call_target="tpu_custom_call" | custom-call | tf_op jit(solution)/shard_map/pool_exchange/pallas_call | solution.py:560
  62.6 8.1 %bev_block.1 = bf16[8,128,256]{2,1,0:T(8,128)(2,1)} custom-call(bf16[16,8,8,256]{3,2,1,0:T(8,128)(2,1)} %get-tuple-element.8.grid_ref, bf16[16,8,256]{2,1,0:T(8,128)(2,1)} %get-tuple-element.9.low_ref, bf16[16,8,256]{2,1,0:T(8,128)(2,1)} %get-tuple-element.10.high_ref, f32[9,256]{1,0:T(8,128)} %tap_ref.1, bf16[256,768]{1,0:T(8,128)(2,1)} %qkv_ref.3, ...), custom_call_target="tpu_custom_call" | custom-call | tf_op jit(solution)/shard_map/bev_block/pallas_call | solution.py:656

commit v2 on v1

--- a/solution.py
+++ b/solution.py
@@ -13,6 +13,8 @@
 CB = 8
 LANES = 128
 CHUNK = 8
+HEADER = 8
+VMEM_LIMIT = 56 * 1024 * 1024
 GROUP = 4
 
 
@@ -185,7 +187,10 @@
     split = jnp.where(single, slots, size_a * CHUNK)
     end_b = jnp.where(single, 0, split + count_b)
     bins = jnp.broadcast_to(pairs + alone, (1, lanes))
-    return jnp.concatenate([win_a, size_a, source_b, win_b, split, count_a, end_b, bins], axis=0)
+    chunk = lax.broadcasted_iota(jnp.int32, (chunks, lanes), 0)
+    sources = jnp.where(chunk < size_a, win_a * chunks + chunk, source_b + chunk - size_a)
+    blank = jnp.zeros((HEADER - 6, lanes), jnp.int32)
+    return jnp.concatenate([win_a, win_b, split, count_a, end_b, bins, blank, sources], axis=0)
 
 
 def voxel_kernel(
@@ -198,13 +203,15 @@
     down_ref,
     pooled_ref,
     acc,
-    xbuf,
+    x_s,
     table_v,
     table,
     twice,
     mixed_s,
     turned_s,
     target_s,
+    older_s,
+    encoded_s,
     rows_s,
     qv_s,
     out_s,
@@ -214,46 +221,29 @@
     table_sem,
 ):
     width = out_ref.shape[0]
-    slots = cell_ref.shape[1]
+    slots = cell_ref.shape[0]
     chunks = slots // CHUNK
     span = GROUP * slots
     cells = acc.shape[0]
     block = rows_s.shape[0]
 
+    load_x = pltpu.make_async_copy(x_hbm, x_s, x_sem)
+    load_x.start()
     table_v[...] = bin_table(count_ref[...], slots)
     to_table = pltpu.make_async_copy(table_v, table, table_sem)
     to_table.start()
     turn_weights(qkv_ref, out_ref, up_ref, down_ref, qv_s, out_s, up_s, down_s)
-    twice[...] = jnp.concatenate([cell_ref[...], cell_ref[...]], axis=1)
+    cell = cell_ref[...].astype(jnp.float32).T.astype(jnp.int32)
+    twice[...] = jnp.concatenate([cell, cell], axis=1)
     to_table.wait()
-    groups = (table[7, 0] + (GROUP - 1)) // GROUP
-
-    def fetch(g, slot):
-        for k in range(GROUP):
-            b = g * GROUP + k
-            size = table[1, b]
-            at = k * chunks
-            pltpu.make_async_copy(
-                x_hbm.at[pl.ds(table[0, b] * chunks, size)],
-                xbuf.at[slot, pl.ds(at, size)],
-                x_sem.at[slot],
-            ).start()
-            pltpu.make_async_copy(
-                x_hbm.at[pl.ds(table[2, b], chunks - size)],
-                xbuf.at[slot, pl.ds(at + size, chunks - size)],
-                x_sem.at[slot],
-            ).start()
-
-    def fetched(slot):
-        pltpu.make_async_copy(
-            x_hbm.at[pl.ds(0, GROUP * chunks)], xbuf.at[slot], x_sem.at[slot]
-        ).wait()
-
-    fetch(0, 0)
+    groups = (table[5, 0] + (GROUP - 1)) // GROUP
+
     acc[...] = jnp.zeros_like(acc)
     mixed_s[...] = jnp.zeros_like(mixed_s)
     turned_s[...] = jnp.zeros_like(turned_s)
     target_s[...] = jnp.full_like(target_s, -1.0)
+    older_s[...] = jnp.full_like(older_s, -1.0)
+    encoded_s[...] = jnp.zeros_like(encoded_s)
     rows_s[...] = lax.broadcasted_iota(jnp.int32, rows_s.shape, 0).astype(jnp.float32).astype(jnp.bfloat16)
 
     lane = lax.broadcasted_iota(jnp.int32, (1, LANES), 1)
@@ -268,12 +258,12 @@
             pick = []
             for half in range(2):
                 b = g * GROUP + 2 * pair + half
-                split = table[4, b]
+                split = table[2, b]
                 own = twice[pl.ds(table[0, b], 1), :]
-                other = twice[pl.ds(table[3, b], 1), :]
+                other = twice[pl.ds(table[1, b], 1), :]
                 other = pltpu.roll(other, lax.rem(split, slots), 1)
                 pick.append(
-                    (split, table[5, b], table[6, b], jnp.where(place < split, own, other))
+                    (split, table[3, b], table[4, b], jnp.where(place < split, own, other))
                 )
             split, count, end, cell = [jnp.where(first, u, v) for u, v in zip(*pick)]
             late = place >= split
@@ -284,56 +274,63 @@
             targets.append(jnp.where(live, cell, -1).astype(jnp.float32))
         return limits, jnp.concatenate(targets, axis=1)
 
-    def step(g, carry):
-        slot = lax.rem(g, 2)
-        fetch(g + 1, 1 - slot)
-        fetched(slot)
-        limits, next_target = limits_of(g)
-
-        def bias_of(pair):
-            low, high = limits[pair]
-            return jnp.where(jnp.logical_and(key_row >= low, key_row < high), 0.0, -1e30)
-
-        mixer = Mixer(span, width, bias_of)
-        target = target_s[...]
+    blocks = cells // block
+
+    def pool(some):
+        target = older_s[...]
+        encoded = encoded_s[...]
         one, none = jnp.bfloat16(1), jnp.bfloat16(0)
-
-        def pool(c):
+        for c in some:
             near = (target - float(c * block)).astype(jnp.bfloat16)
             hot = jnp.where(rows_s[...] == near, one, none)
             at = slice(c * block, (c + 1) * block)
             acc[at, :] += dot(hot, encoded)
 
-        x = xbuf[slot].astype(jnp.float32).reshape(span, width)
+    def step(g, carry):
+        limits, next_target = limits_of(g)
+
+        def bias_of(pair):
+            low, high = limits[pair]
+            return jnp.where(jnp.logical_and(key_row >= low, key_row < high), 0.0, -1e30)
+
+        mixer = Mixer(span, width, bias_of)
+        third = -(-blocks // 3)
+        picks = []
+        for k in range(GROUP):
+            for c in range(chunks):
+                picks.append(x_s[table[HEADER + c, g * GROUP + k]])
+        x = jnp.concatenate([p.astype(jnp.float32) for p in picks], axis=0)
         x_b = x.astype(jnp.bfloat16)
         units = mixer.units
+        projected = dot(out_s[...], mixed_s[...])
         mixer.turn(x_b, qv_s[...])
-        projected = dot(out_s[...], mixed_s[...])
+        hidden = layer_norm(turned_s[...].astype(jnp.float32) + projected, 0).astype(jnp.bfloat16)
         mixer.key(x_b, qkv_ref[:, width : 2 * width])
-        mixer.score(units[0])
-        hidden = layer_norm(turned_s[...].astype(jnp.float32) + projected, 0).astype(jnp.bfloat16)
         turned_s[...] = x.T.astype(jnp.bfloat16)
         lifted = jax.nn.relu(dot(up_s[...], hidden)).astype(jnp.bfloat16)
+        mixer.score(units[0])
+        lowered = dot(down_s[...], lifted)
         mixer.score(units[1])
         mixer.mix(units[0])
-        lowered = dot(down_s[...], lifted)
+        pool(range(0, third))
+        encoded = layer_norm(hidden.astype(jnp.float32) + lowered, 0)
         mixer.score(units[2])
         mixer.mix(units[1])
-        encoded = layer_norm(hidden.astype(jnp.float32) + lowered, 0).T.astype(jnp.bfloat16)
+        pool(range(third, 2 * third))
         mixer.score(units[3])
         mixer.mix(units[2])
-        blocks = cells // block
-        for c in range(blocks // 2):
-            pool(c)
+        pool(range(2 * third, blocks))
         mixer.mix(units[3])
-        for c in range(blocks // 2, blocks):
-            pool(c)
+        target = target_s[...]
+        older_s[...] = target
         target_s[...] = next_target
+        encoded_s[...] = encoded.T.astype(jnp.bfloat16)
         mixed_s[...] = mixer.mixed()
         return carry
 
+    load_x.wait()
     lax.fori_loop(0, groups + 1, step, 0)
-    fetched(lax.rem(groups + 1, 2))
+    pool(range(blocks))
     pooled_ref[...] = acc[...].astype(jnp.bfloat16)
 
 
@@ -350,22 +347,25 @@
         out_shape=jax.ShapeDtypeStruct((cells, width), jnp.bfloat16),
         scratch_shapes=[
             pltpu.VMEM((cells, width), jnp.float32),
-            pltpu.VMEM((2, GROUP * chunks, CHUNK, width), jnp.bfloat16),
-            pltpu.VMEM((8, 2 * windows), jnp.int32),
-            pltpu.SMEM((8, 2 * windows), jnp.int32),
+            pltpu.VMEM((windows * chunks, CHUNK, width), jnp.bfloat16),
+            pltpu.VMEM((HEADER + chunks, 2 * windows), jnp.int32),
+            pltpu.SMEM((HEADER + chunks, 2 * windows), jnp.int32),
             pltpu.VMEM((windows, 2 * slots), jnp.int32),
             pltpu.VMEM((width, span), jnp.bfloat16),
             pltpu.VMEM((width, span), jnp.bfloat16),
             pltpu.VMEM((1, span), jnp.float32),
+            pltpu.VMEM((1, span), jnp.float32),
+            pltpu.VMEM((span, width), jnp.bfloat16),
             pltpu.VMEM((block, span), jnp.bfloat16),
         ]
         + turned_scratch(*weights)
-        + [pltpu.SemaphoreType.DMA((2,)), pltpu.SemaphoreType.DMA],
+        + [pltpu.SemaphoreType.DMA, pltpu.SemaphoreType.DMA],
+        compiler_params=pltpu.CompilerParams(vmem_limit_bytes=VMEM_LIMIT),
         name="voxel_pool",
     )(
         counts.reshape(1, windows),
         feat.reshape(windows * chunks, CHUNK, width),
-        cell,
+        cell.T,
         *weights,
     )
 
@@ -462,17 +462,17 @@
         mine = pooled_ref[pl.ds(j * per, per), band].astype(jnp.float32)
         total = mine + came[j].astype(jnp.float32)
         normal = layer_norm(total).reshape(per, WSIDE, CB, width).astype(jnp.bfloat16)
+        ready[pl.ds(j * per, per)] = normal
         for d in range(per):
-            dest = j * per + d
+            dest = j * per + lax.rem(tile + 1 + d, per)
 
             @pl.when(dest != tile)
             def _():
-                ready[dest] = normal[d]
                 deliver(dest, tile).start()
 
             @pl.when(dest == tile)
             def _():
-                landed[tile] = normal[d]
+                landed[tile] = ready[tile]
 
     def swap_start(i, carry):
         swap(place(i)).start()

time: 71.4 us -> 65 us (0.910)
  Pallas kernels: 69.1 us -> 63.9 us
  local copies, waits for them, and re-layouts: 1.49 us -> 0 us
    pallas_call x1, Pallas kernels: 35.9 us -> 31.8 us  [voxel_pool(): pl.pallas_call(voxel_kernel, in_specs=[vmem, pl.BlockSpec(memory_space=pl...]
    unnamed x1 -> x0, local copies, waits for them, and re-layouts: 1.49 us -> none
    pallas_call x1, Pallas kernels: 25.2 us -> 24 us  [pool_exchange(): pl.pallas_call(functools.partial(pool_kernel, n_tile, n_band), in_specs=[...]
where the time goes in v2:
time: 65 us; the launch traced here: 63.9 us
  Pallas kernels  63.9 us (98%)
    pallas_call x1, Pallas kernels, voxel_pool(): pl.pallas_call(voxel_kernel, in_specs=[vmem, pl.BlockSpec(memory_space=pl...  31.8 us
    pallas_call x1, Pallas kernels, pool_exchange(): pl.pallas_call(functools.partial(pool_kernel, n_tile, n_band), in_specs=[...  24 us
    pallas_call x1, Pallas kernels, bev_block(): pl.pallas_call(bev_kernel, grid=(cols // span,), in_specs=[whole(a) for a...  8.06 us

profile of v2, /device:TPU:11, one launch (start us, length us, event | category | flops | bytes accessed | tf_op | source)
XLA Modules:
  0.0 63.9 jit_solution(6164201190789191040)
XLA Ops:
  0.0 31.8 %voxel_pool.1 = bf16[2048,256]{1,0:T(8,128)(2,1)} custom-call(s32[1,128]{1,0:T(1,128)} %bitcast.7, bf16[1024,8,256]{2,1,0:T(8,128)(2,1)} %bitcast.5, s32[64,128]{1,0:T(8,128)} %bitcast.6, bf16[256,768]{1,0:T(8,128)(2,1)} %qkv_ref.2, bf16[256,256]{1,0:T(8,128)(2,1)} %out_ref.2, bf16[256,512]{1,0:T(8,128)(2,1)} %up_ref.2, bf16[512,256]{1,0:T(8,128)(2,1)} %down_ref.2), custom_call_target="tpu_custom_call" | custom-call | tf_op jit(solution)/shard_map/voxel_pool/pallas_call | solution.py:343
  31.8 24.0 %pool_exchange.1 = (bf16[16,8,8,256]{3,2,1,0:T(8,128)(2,1)}, bf16[16,8,256]{2,1,0:T(8,128)(2,1)}, bf16[16,8,256]{2,1,0:T(8,128)(2,1)}) custom-call(bf16[16,2,64,256]{3,2,1,0:T(8,128)(2,1)} %bitcast.4), custom_call_target="tpu_custom_call" | custom-call | tf_op jit(solution)/shard_map/pool_exchange/pallas_call | solution.py:560
  55.9 8.1 %bev_block.1 = bf16[8,128,256]{2,1,0:T(8,128)(2,1)} custom-call(bf16[16,8,8,256]{3,2,1,0:T(8,128)(2,1)} %get-tuple-element.8.grid_ref, bf16[16,8,256]{2,1,0:T(8,128)(2,1)} %get-tuple-element.9.low_ref, bf16[16,8,256]{2,1,0:T(8,128)(2,1)} %get-tuple-element.10.high_ref, f32[9,256]{1,0:T(8,128)} %tap_ref.1, bf16[256,768]{1,0:T(8,128)(2,1)} %qkv_ref.3, ...), custom_call_target="tpu_custom_call" | custom-call | tf_op jit(solution)/shard_map/bev_block/pallas_call | solution.py:656
